TPU v7x, 32 devices: a whole 2x2x4 slice. The times are simulated.
32 devices in a mesh: group: 2 (over y), tile: 4 (over x, core), seq: 4 (over z).
Axes of the slice: x: 2, y: 2, z: 4, core: 2. Of those that a mesh axis runs over, the one named last changes fastest.
Arguments:
- hidden: bfloat16 [8, 1024, 3072], P(('group', 'tile'), 'seq'), parts along dimension 0
- modulation: float32 [10, 3072], P('group'), parts along dimension 0, may hold values from -3 to 3
- w_qkv: bfloat16 [3072, 9216], P('tile', 'seq')
- w_out: bfloat16 [3072, 3072], P('seq', 'tile'), may hold values from -0.109375 to 0.109375
- w_head: bfloat16 [3072, 64], replicated, may hold values from -0.109375 to 0.109375
- latent: float32 [8, 1024, 64], P(('group', 'tile'), 'seq'), parts along dimension 0, may hold values from -6 to 6
- weights_int: int32 [8, 1024], P(('group', 'tile'), 'seq'), parts along dimension 0, may hold values from 1 to 8
- step_index: int32 [2], P('group'), parts along dimension 0, may hold values from 0 to 13
Outputs:
- stepped: float32 [8, 1024, 64], P(('group', 'tile'), 'seq'), parts along dimension 0
- clean: float32 [8, 1024, 64], P(('group', 'tile'), 'seq'), parts along dimension 0
There are 2 independent parts, one for each index of `group`. A program takes and returns all parts, laid end to end along the dimension named above; an argument that names none is the same for every part. Nothing has to cross between parts.
All inputs are finite; a program needn't handle non-finite values.
Results may differ from a plain program's by a relative error of at most 0.0055.
Values may be sent and summed in bfloat16 or wider, within the bound.
A program may use at most 64 MiB of HBM per device.

v0:
```python
import math
import jax
import jax.numpy as jnp
from jax import lax
from jax.sharding import PartitionSpec as P

HD = 128
NSTEPS = 28


def shifted(value, axis, steps):
    count = lax.axis_size(axis)
    leading, last = (max(0, -steps), min(count, count - steps))
    return lax.ppermute(value, axis, [(source, source + steps) for source in range(leading, last)])


def layer_norm(values):
    mean = jnp.mean(values, axis=-1, keepdims=True)
    centred = values - mean
    spread = jnp.mean(centred * centred, axis=-1, keepdims=True)
    return centred * lax.rsqrt(spread + 1e-06)


def root_norm(values):
    return values * lax.rsqrt(jnp.mean(values * values, axis=-1, keepdims=True) + 1e-06)


def noise_level(index, steps):
    level = 1.0 - index / steps
    return 3.0 * level / (1.0 + 2.0 * level)


def shards(hidden, modulation, w_qkv, w_out, w_head, latent, weights_int, step_index):
    local = hidden[0].astype(jnp.float32)
    norm_in = (layer_norm(local) * (1.0 + modulation[1]) + modulation[0]).astype(jnp.bfloat16)
    gathered = lax.all_gather(norm_in, "seq", axis=0, tiled=True)
    length = gathered.shape[0]
    heads_here = w_qkv.shape[1] // (3 * HD)
    projected = jnp.dot(
        gathered,
        lax.all_gather(w_qkv, "tile", axis=0, tiled=True),
        preferred_element_type=jnp.float32,
    )
    full_out = lax.all_gather(w_out, "tile", axis=1, tiled=True)
    projected = projected.reshape(length, heads_here, 3, HD)
    queries = root_norm(projected[:, :, 0]).astype(jnp.bfloat16)
    keys = root_norm(projected[:, :, 1]).astype(jnp.bfloat16)
    values = projected[:, :, 2].astype(jnp.bfloat16)
    block = min(512, length)
    scale = 1.0 / math.sqrt(HD)
    pieces = []
    for first in range(0, length, block):
        scores = (
            jnp.einsum(
                "qhe,khe->hqk",
                queries[first : first + block],
                keys,
                preferred_element_type=jnp.float32,
            )
            * scale
        )
        expo = jnp.exp(scores)
        probs = (expo / jnp.sum(expo, axis=-1, keepdims=True)).astype(jnp.bfloat16)
        pieces.append(
            jnp.einsum("hqk,khe->qhe", probs, values, preferred_element_type=jnp.float32).astype(
                jnp.bfloat16
            )
        )
    attended = jnp.concatenate(pieces, axis=0).reshape(length, heads_here * HD)
    summed = lax.psum_scatter(
        jnp.dot(attended, full_out, preferred_element_type=jnp.float32).astype(jnp.bfloat16),
        "seq",
        scatter_dimension=0,
        tiled=True,
    ).astype(jnp.float32)
    mixed = local + modulation[2] * summed
    norm_out = (layer_norm(mixed) * (1.0 + modulation[4]) + modulation[3]).astype(jnp.bfloat16)
    velocity = jnp.dot(norm_out, w_head, preferred_element_type=jnp.float32)
    index = step_index[0].astype(jnp.float32)
    now = noise_level(index, NSTEPS)
    after = noise_level(index + 1.0, NSTEPS)
    base = latent[0]
    weight = weights_int[0].astype(jnp.float32)
    moved = base + (after - now) * velocity
    guess = base - now * velocity
    weighted = jnp.concatenate([moved, guess], axis=1) * weight[:, None]
    seq_count = lax.axis_size("seq")
    place = lax.axis_index("seq")
    prev_tile = (
        shifted(weighted.astype(jnp.bfloat16), "tile", 1).astype(weighted.dtype),
        shifted(weight.astype(jnp.bfloat16), "tile", 1).astype(weight.dtype),
    )
    prev_sums, prev_weight = (
        shifted(prev_tile[0].astype(jnp.bfloat16), "seq", -(seq_count - 2)).astype(jnp.float32),
        shifted(prev_tile[1].astype(jnp.bfloat16), "seq", -(seq_count - 2)).astype(jnp.float32),
    )
    next_tile = (
        shifted(weighted.astype(jnp.bfloat16), "tile", -1).astype(weighted.dtype),
        shifted(weight.astype(jnp.bfloat16), "tile", -1).astype(weight.dtype),
    )
    next_sums, next_weight = (
        shifted(next_tile[0].astype(jnp.bfloat16), "seq", seq_count - 2).astype(jnp.float32),
        shifted(next_tile[1].astype(jnp.bfloat16), "seq", seq_count - 2).astype(jnp.float32),
    )
    take_prev = place < 2
    take_next = place >= seq_count - 2
    totals = weighted + jnp.where(take_prev, prev_sums, 0.0) + jnp.where(take_next, next_sums, 0.0)
    norms = weight + jnp.where(take_prev, prev_weight, 0.0) + jnp.where(take_next, next_weight, 0.0)
    joined = totals / norms[:, None]
    channels = velocity.shape[1]
    return (joined[None, :, :channels], joined[None, :, channels:])


def solution(mesh):
    in_specs = (
        P(("group", "tile"), "seq", None),
        P("group", None),
        P("tile", "seq"),
        P("seq", "tile"),
        P(),
        P(("group", "tile"), "seq", None),
        P(("group", "tile"), "seq"),
        P("group"),
    )
    out_specs = (P(("group", "tile"), "seq", None), P(("group", "tile"), "seq", None))
    return jax.shard_map(shards, mesh=mesh, in_specs=in_specs, out_specs=out_specs, check_vma=False)
```

profile of v0, /device:TPU:26, one launch (start us, length us, event | category | flops | bytes accessed | tf_op | source)
XLA Modules:
  0.0 437.2 jit_solution(16859526870282650366)
XLA Ops:
  7.2 0.0 copy-start
  7.2 0.0 copy-start.1
  7.2 0.0 all-gather.4.cloned.1.call-start
  7.2 1.9 fusion.30
  9.1 1.7 convert_reduce_fusion
  10.8 2.0 fusion.8
  12.8 0.0 copy-done.1
  12.8 1.9 fusion.11
  14.7 0.0 all-gather.4.cloned.1.call-update
  14.8 0.0 all-gather.6.cloned.1.call-start
  14.8 0.7 all-gather.6.cloned.1.call-update
  15.5 0.0 all-gather.8.cloned.1.call-start
  15.6 0.7 all-gather.8.cloned.1.call-update
  16.3 0.0 reduce-scatter.2.cloned.1.call-start
  16.3 112.1 %all-gather.4.cloned.1.call-done = bf16[1024,3072]{1,0:T(8,128)(2,1)} async-done(((bf16[256,3072]{1,0:T(8,128)(2,1)}), bf16[1024,3072]{1,0:T(8,128)(2,1)}) %all-gather.4.cloned.1.call-update) | async-done | bytes 6291472 | tf_op jit(solution)/shard_map/all_gather | solution.py:36
  128.4 92.7 %all-gather.6.cloned.1.call-done = bf16[3072,2304]{1,0:T(8,128)(2,1)} async-done(((bf16[768,2304]{1,0:T(8,128)(2,1)}), bf16[3072,2304]{1,0:T(8,128)(2,1)}) %all-gather.6.cloned.1.call-update) | async-done | bytes 14155792 | tf_op jit(solution)/shard_map/all_gather | solution.py:41
  221.1 19.6 %fusion.31 = f32[1024,2304]{0,1:T(8,128)S(1)} fusion(bf16[1024,3072]{1,0:T(8,128)(2,1)} %all-gather.4.cloned.1.call-done, bf16[3072,2304]{1,0:T(8,128)(2,1)} %all-gather.6.cloned.1.call-done), kind=kOutput, calls=%fused_computation.60 | convolution fusion | flops 14495514624 | bytes 29884416 | tf_op jit(solution)/shard_map/dot_general | solution.py:39
  240.7 0.0 copy-start.3
  240.7 3.5 copy-done.3
  244.2 2.0 slice.50
  246.3 3.6 copy.21
  249.9 2.9 fusion.12
  252.8 2.3 multiply_reduce_fusion.1
  255.2 0.0 copy-done.2
  255.2 0.0 slice-start
  255.2 1.0 fusion.13
  256.2 0.0 slice-start.1
  256.2 0.0 slice-start.2
  256.2 8.2 %fusion = (f32[6,512]{1,0:T(8,128)S(1)}, f32[6,512,1024]{2,1,0:T(8,128)}) fusion(f32[1024,6,3,128]{0,3,2,1:T(8,128)} %bitcast.78, f32[1024,6]{0,1:T(8,128)S(1)} %add_rsqrt_fusion, bf16[1024,6,128]{2,0,1:T(8,128)(2,1)S(1)} %fusion.13), kind=kOutput, calls=%fused_computation.4 | convolution fusion | flops 813167616 | bytes 16560128 | tf_op jit(solution)/shard_map/qhe,khe->hqk/dot_general | solution.py:54
  264.4 0.0 slice-done
  264.4 0.0 slice-done.1
  264.4 0.0 slice-done.2
  264.5 2.7 fusion.1
  267.1 6.0 %fusion.19 = bf16[512,6,128]{0,2,1:T(8,128)(2,1)S(1)} fusion(f32[6,512,1024]{2,1,0:T(8,128)} %get-tuple-element.14, f32[6,512]{1,0:T(8,128)S(1)} %get-tuple-element.13, f32[1024,6,3,128]{0,3,2,1:T(8,128)S(1)} %bitcast.82), kind=kOutput, calls=%fused_computation.35 | convolution fusion | flops 815136768 | bytes 14958592 | tf_op jit(solution)/shard_map/hqk,khe->qhe/dot_general | solution.py:65
  273.1 2.9 fusion.20
  276.1 0.2 pad_maximum_fusion
  276.3 0.0 all-gather.8.cloned.1.call-done
  276.3 9.5 %convolution_convert_fusion = bf16[1024,3072]{1,0:T(8,128)(2,1)} fusion(bf16[1024,768]{0,1:T(8,128)(2,1)S(1)} %bitcast.84, bf16[768,3072]{1,0:T(8,128)(2,1)} %all-gather.8.cloned.1.call-done), kind=kOutput, calls=%fused_computation.8 | convolution fusion | flops 4834983936 | bytes 12582912 | tf_op jit(solution)/shard_map/dot_general | solution.py:71
  285.9 0.0 reduce-scatter.2.cloned.1.call-update
  286.5 0.0 copy-done.7
  286.6 110.6 %reduce-scatter.2.cloned.1.call-done = bf16[256,3072]{1,0:T(8,128)(2,1)} async-done(((bf16[1024,3072]{1,0:T(8,128)(2,1)}), bf16[256,3072]{1,0:T(8,128)(2,1)}) %reduce-scatter.2.cloned.1.call-update) | async-done | bytes 1572880 | tf_op jit(solution)/shard_map/reduce_scatter | solution.py:70
  397.2 2.1 fusion.14
  399.4 0.8 multiply_reduce_fusion
  400.2 0.0 copy-done.5
  400.2 0.0 copy-done.6
  400.2 0.0 copy-done.8
  400.2 1.1 bitcast_add_fusion
  401.3 1.9 collective-permute-start
  403.3 3.6 collective-permute-start.2
  406.9 1.9 collective-permute-start.4
  408.9 3.6 collective-permute-start.6
  412.5 0.0 collective-permute-done.4
  412.5 2.9 collective-permute-start.5
  415.5 0.0 collective-permute-done.6
  415.5 1.3 collective-permute-start.7
  416.8 0.0 collective-permute-done
  416.8 5.4 %collective-permute-start.1 = (bf16[256,128]{0,1:T(8,128)(2,1)S(1)}, bf16[256,128]{0,1:T(8,128)(2,1)S(1)}, u32[]{:S(2)}, u32[]{:S(2)}) collective-permute-start(bf16[256,128]{0,1:T(8,128)(2,1)S(1)} %collective-permute-done), channel_id=1, source_target_pairs={{2,0},{3,1},{6,4},{7,5},{10,8},{11,9},{14,12},{15,13},{18,16},{19,... | collective-permute-start | bytes 196616 | tf_op jit(solution)/shard_map/ppermute | solution.py:14
  422.2 0.0 collective-permute-done.2
  422.2 1.3 collective-permute-start.3
  423.5 0.0 collective-permute-done.5
  423.6 0.0 collective-permute-done.7
  423.6 0.5 collective-permute-done.1
  424.1 5.9 %collective-permute-done.3 = bf16[256,128]{0,1:T(8,128)(2,1)S(1)} collective-permute-done((bf16[256,128]{0,1:T(8,128)(2,1)S(1)}, bf16[256,128]{0,1:T(8,128)(2,1)S(1)}, u32[]{:S(2)}, u32[]{:S(2)}) %collective-permute-start.3) | collective-permute-done | bytes 65568 | tf_op jit(solution)/shard_map/ppermute | solution.py:14
  430.0 0.7 slice_bitcast_fusion.1
  (20 shorter events, 0.1 us)
Async XLA Ops:
  7.2 393.0 %copy-start = (bf16[3072,64]{0,1:T(8,128)(2,1)S(1)}, bf16[3072,64]{0,1:T(8,128)(2,1)}, u32[]{:S(2)}) copy-start(bf16[3072,64]{0,1:T(8,128)(2,1)} %param.12) | copy-start | bytes 1179652
  7.2 5.6 %copy-start.1 = (bf16[1,256,3072]{2,1,0:T(8,128)(2,1)S(1)}, bf16[1,256,3072]{2,1,0:T(8,128)(2,1)}, u32[]{:S(2)}) copy-start(bf16[1,256,3072]{2,1,0:T(8,128)(2,1)} %param.8) | copy-start | bytes 4718596
  7.2 121.2 %all-gather.4.cloned.1.call-start = ((), (), s32[]{:S(2)}) async-start(), calls=%async_computation.1 | async-start | bytes 7864320 | tf_op jit(solution)/shard_map/all_gather | solution.py:36
  14.8 206.3 %all-gather.6.cloned.1.call-start = ((), (), s32[]{:S(2)}) async-start(), calls=%async_computation.2 | async-start | bytes 17694720 | tf_op jit(solution)/shard_map/all_gather | solution.py:41
  15.5 260.8 %all-gather.8.cloned.1.call-start = ((), (), s32[]{:S(2)}) async-start(), calls=%async_computation.3 | async-start | bytes 5898240 | tf_op jit(solution)/shard_map/all_gather | solution.py:44
  16.3 381.0 %reduce-scatter.2.cloned.1.call-start = ((), (), s32[]{:S(2)}) async-start(), calls=%async_computation.4 | async-start | bytes 7864320 | tf_op jit(solution)/shard_map/reduce_scatter | solution.py:70
  240.7 3.6 copy-start.3
  249.9 5.3 %copy-start.2 = (f32[1024,6,1,128]{3,0,1,2:T(8,128)S(1)}, f32[1024,6,1,128]{3,0,1,2:T(8,128)}, u32[]{:S(2)}) copy-start(f32[1024,6,1,128]{3,0,1,2:T(8,128)} %copy.21) | copy-start | bytes 9437188
  255.2 9.2 %slice-start = ((s8[9437184]{0:T(1024)(128)(4,1)}), s8[4194304]{0:T(1024)(128)(4,1)S(1)}, s32[]{:S(2)}) async-start(s8[9437184]{0:T(1024)(128)(4,1)} %bitcast.79), calls=%async_computation.5 | async-start | bytes 8388608
  256.2 8.3 %slice-start.1 = ((s8[9437184]{0:T(1024)(128)(4,1)}), s8[4194304]{0:T(1024)(128)(4,1)S(1)}, s32[]{:S(2)}) async-start(s8[9437184]{0:T(1024)(128)(4,1)} %bitcast.79), calls=%async_computation.6 | async-start | bytes 8388608
  256.2 8.2 %slice-start.2 = ((s8[9437184]{0:T(1024)(128)(4,1)}), s8[1048576]{0:T(1024)(128)(4,1)S(1)}, s32[]{:S(2)}) async-start(s8[9437184]{0:T(1024)(128)(4,1)} %bitcast.79), calls=%async_computation.7 | async-start | bytes 2097152
  285.8 0.7 copy-start.7
  397.2 2.1 copy-start.4
  397.2 3.0 copy-start.5
  397.2 3.0 copy-start.6
  397.2 3.0 copy-start.8
  401.3 15.4 %collective-permute-start = (bf16[256,128]{0,1:T(8,128)(2,1)S(1)}, bf16[256,128]{0,1:T(8,128)(2,1)S(1)}, u32[]{:S(2)}, u32[]{:S(2)}) collective-permute-start(bf16[256,128]{0,1:T(8,128)(2,1)S(1)} %fusion.27), channel_id=1, source_target_pairs={{0,4},{4,8},{8,12},{1,5},{5,9},{9,13},{2,6},{6,10},{10,14},{3,7},{... | collective-permute-start | bytes 196616 | tf_op jit(solution)/shard_map/ppermute | solution.py:14
  403.3 19.0 %collective-permute-start.2 = (bf16[256,128]{0,1:T(8,128)(2,1)S(1)}, bf16[256,128]{0,1:T(8,128)(2,1)S(1)}, u32[]{:S(2)}, u32[]{:S(2)}) collective-permute-start(bf16[256,128]{0,1:T(8,128)(2,1)S(1)} %fusion.27), channel_id=1, source_target_pairs={{4,0},{8,4},{12,8},{5,1},{9,5},{13,9},{6,2},{10,6},{14,10},{7,3},{... | collective-permute-start | bytes 196616 | tf_op jit(solution)/shard_map/ppermute | solution.py:14
  406.9 5.6 %collective-permute-start.4 = (bf16[256]{0:T(256)(128)(2,1)S(1)}, bf16[256]{0:T(256)(128)(2,1)S(1)}, u32[]{:S(2)}, u32[]{:S(2)}) collective-permute-start(bf16[256]{0:T(256)(128)(2,1)S(1)} %convert_element_type.109), channel_id=1, source_target_pairs={{0,4},{4,8},{8,12},{1,5},{5,9},{9,13},{2,6},{6,10},{10,14},{3,7},{... | collective-permute-start | bytes 1544 | tf_op jit(solution)/shard_map/ppermute | solution.py:14
  408.9 6.6 %collective-permute-start.6 = (bf16[256]{0:T(256)(128)(2,1)S(1)}, bf16[256]{0:T(256)(128)(2,1)S(1)}, u32[]{:S(2)}, u32[]{:S(2)}) collective-permute-start(bf16[256]{0:T(256)(128)(2,1)S(1)} %convert_element_type.109), channel_id=1, source_target_pairs={{4,0},{8,4},{12,8},{5,1},{9,5},{13,9},{6,2},{10,6},{14,10},{7,3},{... | collective-permute-start | bytes 1544 | tf_op jit(solution)/shard_map/ppermute | solution.py:14
  412.5 11.0 %collective-permute-start.5 = (bf16[256]{0:T(256)(128)(2,1)S(1)}, bf16[256]{0:T(256)(128)(2,1)S(1)}, u32[]{:S(2)}, u32[]{:S(2)}) collective-permute-start(bf16[256]{0:T(256)(128)(2,1)S(1)} %collective-permute-done.4), channel_id=1, source_target_pairs={{2,0},{3,1},{6,4},{7,5},{10,8},{11,9},{14,12},{15,13},{18,16},{19,... | collective-permute-start | bytes 1544 | tf_op jit(solution)/shard_map/ppermute | solution.py:14
  415.5 8.1 %collective-permute-start.7 = (bf16[256]{0:T(256)(128)(2,1)S(1)}, bf16[256]{0:T(256)(128)(2,1)S(1)}, u32[]{:S(2)}, u32[]{:S(2)}) collective-permute-start(bf16[256]{0:T(256)(128)(2,1)S(1)} %collective-permute-done.6), channel_id=1, source_target_pairs={{0,2},{1,3},{4,6},{5,7},{8,10},{9,11},{12,14},{13,15},{16,18},{17,... | collective-permute-start | bytes 1544 | tf_op jit(solution)/shard_map/ppermute | solution.py:14
  416.8 7.3 %collective-permute-start.1 = (bf16[256,128]{0,1:T(8,128)(2,1)S(1)}, bf16[256,128]{0,1:T(8,128)(2,1)S(1)}, u32[]{:S(2)}, u32[]{:S(2)}) collective-permute-start(bf16[256,128]{0,1:T(8,128)(2,1)S(1)} %collective-permute-done), channel_id=1, source_target_pairs={{2,0},{3,1},{6,4},{7,5},{10,8},{11,9},{14,12},{15,13},{18,16},{19,... | collective-permute-start | bytes 196616 | tf_op jit(solution)/shard_map/ppermute | solution.py:14
  422.2 7.7 %collective-permute-start.3 = (bf16[256,128]{0,1:T(8,128)(2,1)S(1)}, bf16[256,128]{0,1:T(8,128)(2,1)S(1)}, u32[]{:S(2)}, u32[]{:S(2)}) collective-permute-start(bf16[256,128]{0,1:T(8,128)(2,1)S(1)} %collective-permute-done.2), channel_id=1, source_target_pairs={{0,2},{1,3},{4,6},{5,7},{8,10},{9,11},{12,14},{13,15},{16,18},{17,... | collective-permute-start | bytes 196616 | tf_op jit(solution)/shard_map/ppermute | solution.py:14
Sparse Core Ops, SparseCore 0:
  14.9 113.4 all-gather.3
  129.9 91.1 all-gather.5
  222.6 37.4 all-gather.7
  286.0 111.1 reduce-scatter.1
where the time goes:
time: 438 us; the launch traced here: 437 us
  waiting for transfers between devices  323 us (74%)
  matrix products  50 us (11%)
  starting transfers between devices  22.2 us (5%)
  other arithmetic  17 us (4%)
  between operations  14.9 us (3%)
  local copies, waits for them, and re-layouts  9.9 us (2%)
    all_gather x1, waiting for transfers between devices, shards(): gathered = lax.all_gather(norm_in, 'seq', axis=0, tiled=True)  112 us
    reduce_scatter x1, waiting for transfers between devices, shards(): lax.psum_scatter(jnp.dot(attended, full_out, preferred_element_type=jnp.f...  111 us
    all_gather x1, waiting for transfers between devices, shards(): lax.all_gather(w_qkv, 'tile', axis=0, tiled=True)  92.7 us
    ppermute x8, starting transfers between devices, shifted(): lax.ppermute(value, axis, [(source, source + steps) for source in range(l...  22.1 us
    dot_general x1, matrix products, shards(): jnp.dot(gathered, lax.all_gather(w_qkv, 'tile', axis=0, tiled=True), pref...  19.6 us
    dot_general x2, matrix products, shards(): jnp.einsum('qhe,khe->hqk', queries[first:first + block], keys, preferred_...  10.9 us
    dot_general x1, matrix products, shards(): jnp.dot(attended, full_out, preferred_element_type=jnp.float32)  9.54 us
    dot_general x2, matrix products, shards(): jnp.einsum('hqk,khe->qhe', probs, values, preferred_element_type=jnp.floa...  8.92 us
  transfers between devices with their start and end apart: 12, of which 5 were waited for; matrix products, arithmetic and copies ran while one was open for 12% of the time, Pallas kernels for 0%

commit v1 on v0

--- a/solution.py
+++ b/solution.py
@@ -33,7 +33,14 @@
 def shards(hidden, modulation, w_qkv, w_out, w_head, latent, weights_int, step_index):
     local = hidden[0].astype(jnp.float32)
     norm_in = (layer_norm(local) * (1.0 + modulation[1]) + modulation[0]).astype(jnp.bfloat16)
-    gathered = lax.all_gather(norm_in, "seq", axis=0, tiled=True)
+    ways, here, hop = (lax.axis_size("seq"), lax.axis_index("seq"), norm_in.shape[0])
+    line, have = (norm_in, 1)
+    while have < ways:
+        line = jnp.concatenate(
+            [line, lax.ppermute(line, "seq", [(d, (d - have) % ways) for d in range(ways)])], axis=0
+        )
+        have = 2 * have
+    gathered = jnp.roll(line, here * hop, axis=0)
     length = gathered.shape[0]
     heads_here = w_qkv.shape[1] // (3 * HD)
     projected = jnp.dot(

time: 438 us -> 414 us (0.945)
  waiting for transfers between devices: 323 us -> 290 us
  local copies, waits for them, and re-layouts: 9.9 us -> 21.8 us
    ppermute x0 -> x2, waiting for transfers between devices: none -> 172 us  [shards(): lax.ppermute(line, 'seq', [(d, (d - have) % ways) for d in range(ways)])]
    all_gather x1 -> x0, waiting for transfers between devices: 112 us -> none  [shards(): gathered = lax.all_gather(norm_in, 'seq', axis=0, tiled=True)]
    all_gather x1, waiting for transfers between devices: 92.7 us -> 0.01 us  [shards(): lax.all_gather(w_qkv, 'tile', axis=0, tiled=True)]
    unnamed x25 -> x35, local copies, waits for them, and re-layouts: 7.19 us -> 15.3 us
  transfers between devices with their start and end apart: 12 -> 13, of which waited for: 5 -> 5; matrix products, arithmetic and copies ran while one was open for 12% -> 16% of each run, Pallas kernels for 0% -> 0%
where the time goes in v1:
time: 414 us
  waiting for transfers between devices  290 us (70%)
  matrix products  50 us (12%)
  starting transfers between devices  22.7 us (5%)
  local copies, waits for them, and re-layouts  21.8 us (5%)
  between operations  14.9 us (4%)
  other arithmetic  14.7 us (4%)
    ppermute x2, waiting for transfers between devices, shards(): lax.ppermute(line, 'seq', [(d, (d - have) % ways) for d in range(ways)])  172 us
    reduce_scatter x1, waiting for transfers between devices, shards(): lax.psum_scatter(jnp.dot(attended, full_out, preferred_element_type=jnp.f...  111 us
    ppermute x8, starting transfers between devices, shifted(): lax.ppermute(value, axis, [(source, source + steps) for source in range(l...  22.1 us
    dot_general x1, matrix products, shards(): jnp.dot(gathered, lax.all_gather(w_qkv, 'tile', axis=0, tiled=True), pref...  19.6 us
    unnamed x35, local copies, waits for them, and re-layouts  15.3 us
    dot_general x2, matrix products, shards(): jnp.einsum('qhe,khe->hqk', queries[first:first + block], keys, preferred_...  10.9 us
    dot_general x1, matrix products, shards(): jnp.dot(attended, full_out, preferred_element_type=jnp.float32)  9.6 us
    dot_general x2, matrix products, shards(): jnp.einsum('hqk,khe->qhe', probs, values, preferred_element_type=jnp.floa...  8.92 us
  transfers between devices with their start and end apart: 13, of which 5 were waited for; matrix products, arithmetic and copies ran while one was open for 16% of the time, Pallas kernels for 0%

profile of v1, /device:TPU:26, one launch (start us, length us, event | category | flops | bytes accessed | tf_op | source)
XLA Modules:
  0.0 413.9 jit_solution(17452144946436750811)
XLA Ops:
  7.2 0.0 copy-start
  7.2 0.0 copy-start.1
  7.2 0.0 copy-start.7
  7.2 0.0 all-gather.3.cloned.1.call-start
  7.2 0.7 all-gather.3.cloned.1.call-update
  7.9 0.0 all-gather.5.cloned.1.call-start
  8.0 0.7 copy-done.1
  8.6 0.3 convert_reduce_fusion
  8.9 0.6 fusion.10
  9.5 0.0 copy-done.7
  9.5 0.7 fusion.34
  10.2 1.8 constant_dynamic-update-slice_fusion.5
  12.0 0.4 collective-permute-start
  12.4 37.5 %collective-permute-done = bf16[256,3072]{1,0:T(8,128)(2,1)S(1)} collective-permute-done((bf16[256,3072]{1,0:T(8,128)(2,1)S(1)}, bf16[256,3072]{1,0:T(8,128)(2,1)S(1)}, u32[]{:S(2)}, u32[]{:S(2)}) %collective-permute-start) | collective-permute-done | bytes 1572896 | tf_op jit(solution)/shard_map/ppermute | solution.py:40
  49.9 1.9 pad_maximum_fusion
  51.9 0.0 copy-done.4
  51.9 0.0 collective-permute-start.1
  51.9 0.0 all-gather.5.cloned.1.call-update
  51.9 0.0 reduce-scatter.2.cloned.1.call-start
  52.0 1.2 constant_dynamic-update-slice_fusion.4
  53.2 134.5 %collective-permute-done.1 = bf16[512,3072]{1,0:T(8,128)(2,1)} collective-permute-done((bf16[512,3072]{1,0:T(8,128)(2,1)}, bf16[512,3072]{1,0:T(8,128)(2,1)}, u32[]{:S(2)}, u32[]{:S(2)}) %collective-permute-start.1) | collective-permute-done | bytes 3145760 | tf_op jit(solution)/shard_map/ppermute | solution.py:40
  187.7 3.7 constant_dynamic-update-slice_fusion.3
  191.4 1.3 constant_dynamic-update-slice_fusion.2
  192.7 1.3 constant_dynamic-update-slice_fusion.1
  194.0 3.8 constant_dynamic-update-slice_fusion
  197.7 19.6 %fusion.2 = f32[1024,2304]{0,1:T(8,128)S(1)} fusion(bf16[3072,2304]{1,0:T(8,128)(2,1)} %all-gather.3.cloned.1.call-done, bf16[2048,3072]{1,0:T(8,128)(2,1)} %constant_dynamic-update-slice_fusion, s32[]{:T(128)S(6)} %select_n.42), kind=kOutput, calls=%fused_computation.6 | convolution fusion | flops 14495514624 | bytes 29884420 | tf_op jit(solution)/shard_map/dot_general | solution.py:46
  217.3 3.5 copy-done.3
  220.9 2.1 slice.50
  223.0 3.5 copy.21
  226.5 2.9 fusion.14
  229.5 2.3 multiply_reduce_fusion.1
  231.8 0.0 slice-start
  231.8 1.0 fusion.15
  232.8 0.0 slice-start.1
  232.8 0.0 slice-start.2
  232.8 8.2 %fusion = (f32[6,512]{1,0:T(8,128)S(1)}, f32[6,512,1024]{2,1,0:T(8,128)}) fusion(f32[1024,6,3,128]{0,3,2,1:T(8,128)} %bitcast.78, f32[1024,6]{0,1:T(8,128)S(1)} %add_rsqrt_fusion, bf16[1024,6,128]{2,0,1:T(8,128)(2,1)S(1)} %fusion.15), kind=kOutput, calls=%fused_computation.4 | convolution fusion | flops 813167616 | bytes 16560128 | tf_op jit(solution)/shard_map/qhe,khe->hqk/dot_general | solution.py:61
  241.0 2.7 fusion.1
  243.7 6.0 %fusion.21 = bf16[512,6,128]{0,2,1:T(8,128)(2,1)S(1)} fusion(f32[6,512,1024]{2,1,0:T(8,128)} %get-tuple-element.16, f32[6,512]{1,0:T(8,128)S(1)} %get-tuple-element.15, f32[1024,6,3,128]{0,3,2,1:T(8,128)S(1)} %bitcast.82), kind=kOutput, calls=%fused_computation.38 | convolution fusion | flops 815136768 | bytes 14958592 | tf_op jit(solution)/shard_map/hqk,khe->qhe/dot_general | solution.py:72
  249.7 2.9 fusion.22
  252.6 0.2 pad_maximum_fusion.1
  252.9 0.0 all-gather.5.cloned.1.call-done
  252.9 9.6 %convolution_convert_fusion = bf16[1024,3072]{1,0:T(8,128)(2,1)} fusion(bf16[1024,768]{0,1:T(8,128)(2,1)S(1)} %bitcast.84, bf16[768,3072]{1,0:T(8,128)(2,1)} %all-gather.5.cloned.1.call-done), kind=kOutput, calls=%fused_computation.10 | convolution fusion | flops 4834983936 | bytes 12582912 | tf_op jit(solution)/shard_map/dot_general | solution.py:78
  262.5 0.0 reduce-scatter.2.cloned.1.call-update
  263.3 110.6 %reduce-scatter.2.cloned.1.call-done = bf16[256,3072]{1,0:T(8,128)(2,1)} async-done(((bf16[1024,3072]{1,0:T(8,128)(2,1)}), bf16[256,3072]{1,0:T(8,128)(2,1)}) %reduce-scatter.2.cloned.1.call-update) | async-done | bytes 1572880 | tf_op jit(solution)/shard_map/reduce_scatter | solution.py:77
  373.9 2.1 fusion.16
  376.0 0.8 multiply_reduce_fusion
  376.9 1.1 bitcast_add_fusion
  378.0 1.9 collective-permute-start.2
  379.9 3.6 collective-permute-start.4
  383.6 1.9 collective-permute-start.6
  385.5 3.6 collective-permute-start.8
  389.2 0.0 collective-permute-done.6
  389.2 2.9 collective-permute-start.7
  392.1 0.0 collective-permute-done.8
  392.1 1.3 collective-permute-start.9
  393.4 0.0 collective-permute-done.2
  393.4 5.4 %collective-permute-start.3 = (bf16[256,128]{0,1:T(8,128)(2,1)S(1)}, bf16[256,128]{0,1:T(8,128)(2,1)S(1)}, u32[]{:S(2)}, u32[]{:S(2)}) collective-permute-start(bf16[256,128]{0,1:T(8,128)(2,1)S(1)} %collective-permute-done.2), channel_id=1, source_target_pairs={{2,0},{3,1},{6,4},{7,5},{10,8},{11,9},{14,12},{15,13},{18,16},{19,... | collective-permute-start | bytes 196616 | tf_op jit(solution)/shard_map/ppermute | solution.py:14
  398.9 0.0 collective-permute-done.4
  398.9 1.3 collective-permute-start.5
  400.2 0.0 collective-permute-done.7
  400.2 0.0 collective-permute-done.9
  400.2 0.5 collective-permute-done.3
  400.8 5.9 %collective-permute-done.5 = bf16[256,128]{0,1:T(8,128)(2,1)S(1)} collective-permute-done((bf16[256,128]{0,1:T(8,128)(2,1)S(1)}, bf16[256,128]{0,1:T(8,128)(2,1)S(1)}, u32[]{:S(2)}, u32[]{:S(2)}) %collective-permute-start.5) | collective-permute-done | bytes 65568 | tf_op jit(solution)/shard_map/ppermute | solution.py:14
  406.7 0.7 slice_bitcast_fusion.1
  (33 shorter events, 0.2 us)
Async XLA Ops:
  7.2 369.7 %copy-start = (bf16[3072,64]{0,1:T(8,128)(2,1)S(1)}, bf16[3072,64]{0,1:T(8,128)(2,1)}, u32[]{:S(2)}) copy-start(bf16[3072,64]{0,1:T(8,128)(2,1)} %param.12) | copy-start | bytes 1179652
  7.2 1.5 copy-start.1
  7.2 2.3 copy-start.7
  7.2 190.5 %all-gather.3.cloned.1.call-start = ((), (), s32[]{:S(2)}) async-start(), calls=%async_computation.1 | async-start | bytes 17694720 | tf_op jit(solution)/shard_map/all_gather | solution.py:48
  7.9 244.9 %all-gather.5.cloned.1.call-start = ((), (), s32[]{:S(2)}) async-start(), calls=%async_computation.2 | async-start | bytes 5898240 | tf_op jit(solution)/shard_map/all_gather | solution.py:51
  12.0 39.9 %copy-start.4 = (bf16[256,3072]{1,0:T(8,128)(2,1)}, bf16[256,3072]{1,0:T(8,128)(2,1)S(1)}, u32[]{:S(2)}) copy-start(bf16[256,3072]{1,0:T(8,128)(2,1)S(1)} %get-tuple-element.3) | copy-start | bytes 4718596
  12.0 37.9 %collective-permute-start = (bf16[256,3072]{1,0:T(8,128)(2,1)S(1)}, bf16[256,3072]{1,0:T(8,128)(2,1)S(1)}, u32[]{:S(2)}, u32[]{:S(2)}) collective-permute-start(bf16[256,3072]{1,0:T(8,128)(2,1)S(1)} %get-tuple-element.3), channel_id=1, source_target_pairs={{0,3},{1,0},{2,1},{3,2},{4,7},{5,4},{6,5},{7,6},{8,11},{9,8},{10,9... | collective-permute-start | bytes 4718600 | tf_op jit(solution)/shard_map/ppermute | solution.py:40
  51.9 135.8 %collective-permute-start.1 = (bf16[512,3072]{1,0:T(8,128)(2,1)}, bf16[512,3072]{1,0:T(8,128)(2,1)}, u32[]{:S(2)}, u32[]{:S(2)}) collective-permute-start(bf16[512,3072]{1,0:T(8,128)(2,1)} %pad_maximum_fusion), channel_id=1, source_target_pairs={{0,2},{1,3},{2,0},{3,1},{4,6},{5,7},{6,4},{7,5},{8,10},{9,11},{10,... | collective-permute-start | bytes 9437192 | tf_op jit(solution)/shard_map/ppermute | solution.py:40
  51.9 322.0 %reduce-scatter.2.cloned.1.call-start = ((), (), s32[]{:S(2)}) async-start(), calls=%async_computation.3 | async-start | bytes 7864320 | tf_op jit(solution)/shard_map/reduce_scatter | solution.py:77
  53.2 138.2 %copy-start.5 = (bf16[256,3072]{1,0:T(8,128)(2,1)S(1)}, bf16[256,3072]{1,0:T(8,128)(2,1)}, u32[]{:S(2)}) copy-start(bf16[256,3072]{1,0:T(8,128)(2,1)} %copy-done.4) | copy-start | bytes 4718596
  217.3 3.6 copy-start.3
  226.5 5.3 %copy-start.2 = (f32[1024,6,1,128]{3,0,1,2:T(8,128)S(1)}, f32[1024,6,1,128]{3,0,1,2:T(8,128)}, u32[]{:S(2)}) copy-start(f32[1024,6,1,128]{3,0,1,2:T(8,128)} %copy.21) | copy-start | bytes 9437188
  231.8 9.2 %slice-start = ((s8[9437184]{0:T(1024)(128)(4,1)}), s8[4194304]{0:T(1024)(128)(4,1)S(1)}, s32[]{:S(2)}) async-start(s8[9437184]{0:T(1024)(128)(4,1)} %bitcast.79), calls=%async_computation.4 | async-start | bytes 8388608
  232.8 8.2 %slice-start.1 = ((s8[9437184]{0:T(1024)(128)(4,1)}), s8[4194304]{0:T(1024)(128)(4,1)S(1)}, s32[]{:S(2)}) async-start(s8[9437184]{0:T(1024)(128)(4,1)} %bitcast.79), calls=%async_computation.5 | async-start | bytes 8388608
  232.8 8.2 %slice-start.2 = ((s8[9437184]{0:T(1024)(128)(4,1)}), s8[1048576]{0:T(1024)(128)(4,1)S(1)}, s32[]{:S(2)}) async-start(s8[9437184]{0:T(1024)(128)(4,1)} %bitcast.79), calls=%async_computation.6 | async-start | bytes 2097152
  262.5 0.7 copy-start.10
  373.9 2.1 copy-start.6
  373.9 3.0 copy-start.8
  373.9 3.0 copy-start.9
  373.9 3.0 copy-start.11
  378.0 15.4 %collective-permute-start.2 = (bf16[256,128]{0,1:T(8,128)(2,1)S(1)}, bf16[256,128]{0,1:T(8,128)(2,1)S(1)}, u32[]{:S(2)}, u32[]{:S(2)}) collective-permute-start(bf16[256,128]{0,1:T(8,128)(2,1)S(1)} %fusion.29), channel_id=1, source_target_pairs={{0,4},{4,8},{8,12},{1,5},{5,9},{9,13},{2,6},{6,10},{10,14},{3,7},{... | collective-permute-start | bytes 196616 | tf_op jit(solution)/shard_map/ppermute | solution.py:14
  379.9 19.0 %collective-permute-start.4 = (bf16[256,128]{0,1:T(8,128)(2,1)S(1)}, bf16[256,128]{0,1:T(8,128)(2,1)S(1)}, u32[]{:S(2)}, u32[]{:S(2)}) collective-permute-start(bf16[256,128]{0,1:T(8,128)(2,1)S(1)} %fusion.29), channel_id=1, source_target_pairs={{4,0},{8,4},{12,8},{5,1},{9,5},{13,9},{6,2},{10,6},{14,10},{7,3},{... | collective-permute-start | bytes 196616 | tf_op jit(solution)/shard_map/ppermute | solution.py:14
  383.6 5.6 %collective-permute-start.6 = (bf16[256]{0:T(256)(128)(2,1)S(1)}, bf16[256]{0:T(256)(128)(2,1)S(1)}, u32[]{:S(2)}, u32[]{:S(2)}) collective-permute-start(bf16[256]{0:T(256)(128)(2,1)S(1)} %convert_element_type.109), channel_id=1, source_target_pairs={{0,4},{4,8},{8,12},{1,5},{5,9},{9,13},{2,6},{6,10},{10,14},{3,7},{... | collective-permute-start | bytes 1544 | tf_op jit(solution)/shard_map/ppermute | solution.py:14
  385.5 6.6 %collective-permute-start.8 = (bf16[256]{0:T(256)(128)(2,1)S(1)}, bf16[256]{0:T(256)(128)(2,1)S(1)}, u32[]{:S(2)}, u32[]{:S(2)}) collective-permute-start(bf16[256]{0:T(256)(128)(2,1)S(1)} %convert_element_type.109), channel_id=1, source_target_pairs={{4,0},{8,4},{12,8},{5,1},{9,5},{13,9},{6,2},{10,6},{14,10},{7,3},{... | collective-permute-start | bytes 1544 | tf_op jit(solution)/shard_map/ppermute | solution.py:14
  389.2 11.0 %collective-permute-start.7 = (bf16[256]{0:T(256)(128)(2,1)S(1)}, bf16[256]{0:T(256)(128)(2,1)S(1)}, u32[]{:S(2)}, u32[]{:S(2)}) collective-permute-start(bf16[256]{0:T(256)(128)(2,1)S(1)} %collective-permute-done.6), channel_id=1, source_target_pairs={{2,0},{3,1},{6,4},{7,5},{10,8},{11,9},{14,12},{15,13},{18,16},{19,... | collective-permute-start | bytes 1544 | tf_op jit(solution)/shard_map/ppermute | solution.py:14
  392.1 8.1 %collective-permute-start.9 = (bf16[256]{0:T(256)(128)(2,1)S(1)}, bf16[256]{0:T(256)(128)(2,1)S(1)}, u32[]{:S(2)}, u32[]{:S(2)}) collective-permute-start(bf16[256]{0:T(256)(128)(2,1)S(1)} %collective-permute-done.8), channel_id=1, source_target_pairs={{0,2},{1,3},{4,6},{5,7},{8,10},{9,11},{12,14},{13,15},{16,18},{17,... | collective-permute-start | bytes 1544 | tf_op jit(solution)/shard_map/ppermute | solution.py:14
  393.4 7.3 %collective-permute-start.3 = (bf16[256,128]{0,1:T(8,128)(2,1)S(1)}, bf16[256,128]{0,1:T(8,128)(2,1)S(1)}, u32[]{:S(2)}, u32[]{:S(2)}) collective-permute-start(bf16[256,128]{0,1:T(8,128)(2,1)S(1)} %collective-permute-done.2), channel_id=1, source_target_pairs={{2,0},{3,1},{6,4},{7,5},{10,8},{11,9},{14,12},{15,13},{18,16},{19,... | collective-permute-start | bytes 196616 | tf_op jit(solution)/shard_map/ppermute | solution.py:14
  398.9 7.7 %collective-permute-start.5 = (bf16[256,128]{0,1:T(8,128)(2,1)S(1)}, bf16[256,128]{0,1:T(8,128)(2,1)S(1)}, u32[]{:S(2)}, u32[]{:S(2)}) collective-permute-start(bf16[256,128]{0,1:T(8,128)(2,1)S(1)} %collective-permute-done.4), channel_id=1, source_target_pairs={{0,2},{1,3},{4,6},{5,7},{8,10},{9,11},{12,14},{13,15},{16,18},{17,... | collective-permute-start | bytes 196616 | tf_op jit(solution)/shard_map/ppermute | solution.py:14
Sparse Core Ops, SparseCore 0:
  9.6 91.0 all-gather.2
  102.2 37.4 all-gather.4
  262.6 111.2 reduce-scatter.1
